TPU v7x, 256 devices: a whole 4x4x8 slice. The times are simulated.
256 devices in a mesh: ia: 4 (over y), ja: 8 (over x, core), ka: 8 (over z).
Axes of the slice: x: 4, y: 4, z: 8, core: 2. Of those that a mesh axis runs over, the one named last changes fastest.
Arguments:
- observed: bfloat16 [4, 8, 40, 128, 32, 128], P('ia', 'ja', 'ka'), may hold values from -6 to 6
- weights: bfloat16 [4, 8, 40, 128, 32, 128], P('ia', 'ja', 'ka'), may hold values from 0 to 4, as said below
- coords: int32 [4, 8, 40, 3], P('ia', 'ja', 'ka'), may hold values from 0 to 31, as said below
- counts: int32 [4, 8, 8], P('ia', 'ja', 'ka'), may hold values from 0 to 5, as said below
- factor_rows: bfloat16 [64, 4096], P(None, ('ia', 'ja', 'ka')), may hold values from -0.75 to 0.75
- factor_cols: bfloat16 [64, 4096], P(None, ('ja', 'ka')), may hold values from -0.75 to 0.75
- factor_depth: bfloat16 [64, 1024], replicated, may hold values from -0.75 to 0.75
- core_tensor: bfloat16 [64, 64, 64], replicated, may hold values from -6 to 6
Outputs:
- rows_gradient: float32 [64, 4096], P(None, ('ia', 'ja', 'ka'))
- cols_gradient: float32 [64, 4096], P(None, ('ja', 'ka'))
- depth_gradient: float32 [64, 1024], P(None, 'ka')
- core_gradient: float32 [64, 64, 64], replicated
Inputs may be any that keep to these rules, and one draw needn't show every extreme that they name: counts[a, b, c] is the number of live slots of the device at index a of ia, b of ja, c of ka; the busiest devices hold 5. coords[a, b, c * 5 + s] = (p, q, t) with a * 8 <= p < (a + 1) * 8, b * 4 <= q < (b + 1) * 4, c * 4 <= t < (c + 1) * 4; the 5 slots of one device name distinct blocks. `weights`: zero at unobserved entries, positive at observed ones.
All inputs are finite; a program needn't handle non-finite values.
Results may differ from a plain program's by a relative error of at most 0.0012.
Values may be sent and summed in bfloat16 or wider, within the bound.
A program may use at most 64 MiB of HBM per device.

v0:
```python
import jax
import jax.numpy as jnp
from jax import lax
from jax.sharding import PartitionSpec as P

resid_scale = 1.0 / 64.0


def block_terms(observed_block, weight_block, row_factor, col_factor, depth_factor, core_tensor):
    rank_width, block_rows = row_factor.shape
    block_cols = col_factor.shape[1]
    slab_depth = depth_factor.shape[1]
    core_flat = core_tensor.reshape(rank_width * rank_width, rank_width)
    first_cube = jnp.dot(core_flat, depth_factor, preferred_element_type=jnp.float32).astype(
        jnp.bfloat16
    )
    first_cube = first_cube.reshape(rank_width, rank_width, slab_depth)
    second_cube = jnp.einsum(
        "rsk,sj->rkj", first_cube, col_factor, preferred_element_type=jnp.float32
    ).astype(jnp.bfloat16)
    second_flat = second_cube.reshape(rank_width, slab_depth * block_cols)
    model_block = lax.dot_general(
        row_factor, second_flat, (((0,), (0,)), ((), ())), preferred_element_type=jnp.float32
    )
    weight_flat = weight_block.reshape(block_rows, slab_depth * block_cols).astype(jnp.float32)
    data_flat = observed_block.reshape(block_rows, slab_depth * block_cols).astype(jnp.float32)
    residual = (weight_flat * (model_block - data_flat) * resid_scale).astype(jnp.bfloat16)
    row_term = lax.dot_general(
        second_flat, residual, (((1,), (1,)), ((), ())), preferred_element_type=jnp.float32
    )
    first_back = jnp.dot(row_factor, residual, preferred_element_type=jnp.float32).astype(
        jnp.bfloat16
    )
    back_cube = first_back.reshape(rank_width, slab_depth, block_cols)
    col_term = jnp.einsum("rsk,rkj->sj", first_cube, back_cube, preferred_element_type=jnp.float32)
    second_back = jnp.einsum(
        "sj,rkj->rsk", col_factor, back_cube, preferred_element_type=jnp.float32
    ).astype(jnp.bfloat16)
    back_flat = second_back.reshape(rank_width * rank_width, slab_depth)
    depth_term = lax.dot_general(
        core_flat, back_flat, (((0,), (0,)), ((), ())), preferred_element_type=jnp.float32
    )
    core_term = lax.dot_general(
        back_flat, depth_factor, (((1,), (1,)), ((), ())), preferred_element_type=jnp.float32
    )
    return (row_term, col_term, depth_term, core_term.reshape(rank_width, rank_width, rank_width))


def add_columns(table, piece, start_col):
    width = piece.shape[1]
    return lax.dynamic_update_slice_in_dim(
        table, lax.dynamic_slice_in_dim(table, start_col, width, 1) + piece, start_col, 1
    )


def accumulate_blocks(
    live_count,
    data_slots,
    weight_slots,
    coord_slots,
    row_table,
    col_table,
    factor_depth,
    core_tensor,
    row_base,
    col_base,
):
    rank_width = core_tensor.shape[0]
    block_rows = data_slots.shape[1]
    slab_depth = data_slots.shape[2]
    block_cols = data_slots.shape[3]
    start_sums = (
        jnp.zeros((rank_width, row_table.shape[1]), jnp.float32),
        jnp.zeros((rank_width, col_table.shape[1]), jnp.float32),
        jnp.zeros((rank_width, factor_depth.shape[1]), jnp.float32),
        jnp.zeros((rank_width, rank_width, rank_width), jnp.float32),
    )

    def add_slot(slot_index, running):
        rows_sum, cols_sum, depth_sum, core_sum = running
        position = coord_slots[slot_index]
        row_start = (position[0] - row_base) * block_rows
        col_start = (position[1] - col_base) * block_cols
        depth_start = position[2] * slab_depth
        row_factor = lax.dynamic_slice_in_dim(row_table, row_start, block_rows, 1)
        col_factor = lax.dynamic_slice_in_dim(col_table, col_start, block_cols, 1)
        depth_factor = lax.dynamic_slice_in_dim(factor_depth, depth_start, slab_depth, 1)
        block_sums = block_terms(
            data_slots[slot_index],
            weight_slots[slot_index],
            row_factor,
            col_factor,
            depth_factor,
            core_tensor,
        )
        rows_sum = add_columns(rows_sum, block_sums[0], row_start)
        cols_sum = add_columns(cols_sum, block_sums[1], col_start)
        depth_sum = add_columns(depth_sum, block_sums[2], depth_start)
        return (rows_sum, cols_sum, depth_sum, core_sum + block_sums[3])

    return lax.fori_loop(0, live_count, add_slot, start_sums)


def on_device(
    observed, weights, coords, counts, factor_rows, factor_cols, factor_depth, core_tensor
):
    slot_count = observed.shape[2]
    data_slots = observed.reshape(observed.shape[2:])
    weight_slots = weights.reshape(weights.shape[2:])
    coord_slots = coords.reshape(slot_count, 3)
    own_count = counts.reshape(())
    row_table = lax.all_gather(factor_rows, ("ja", "ka"), axis=1, tiled=True)
    col_table = lax.all_gather(factor_cols, "ka", axis=1, tiled=True)
    row_base = lax.axis_index("ia") * (row_table.shape[1] // observed.shape[3])
    col_base = lax.axis_index("ja") * (col_table.shape[1] // observed.shape[5])
    rows_sum, cols_sum, depth_sum, core_sum = accumulate_blocks(
        own_count,
        data_slots,
        weight_slots,
        coord_slots,
        row_table,
        col_table,
        factor_depth,
        core_tensor,
        row_base,
        col_base,
    )
    rows_gradient = lax.psum_scatter(rows_sum, ("ja", "ka"), scatter_dimension=1, tiled=True)
    cols_whole = lax.psum(cols_sum, "ia")
    depth_whole = lax.psum(depth_sum, ("ia", "ja"))
    cols_gradient, depth_gradient = (
        lax.psum_scatter(cols_whole, "ka", scatter_dimension=1, tiled=True),
        lax.psum_scatter(depth_whole, "ka", scatter_dimension=1, tiled=True),
    )
    core_gradient = lax.psum(core_sum, ("ia", "ja", "ka"))
    return (rows_gradient, cols_gradient, depth_gradient, core_gradient)


def solution(mesh):
    in_specs = (
        P("ia", "ja", "ka", None, None, None),
        P("ia", "ja", "ka", None, None, None),
        P("ia", "ja", "ka", None),
        P("ia", "ja", "ka"),
        P(None, ("ia", "ja", "ka")),
        P(None, ("ja", "ka")),
        P(),
        P(),
    )
    out_specs = (P(None, ("ia", "ja", "ka")), P(None, ("ja", "ka")), P(None, "ka"), P())
    return jax.shard_map(
        on_device, mesh=mesh, in_specs=in_specs, out_specs=out_specs, check_vma=False
    )
```

profile of v0, /device:TPU:2, one launch (start us, length us, event | category | flops | bytes accessed | tf_op | source)
XLA Modules:
  0.0 616.1 jit_solution(5447334796632463020)
XLA Ops:
  8.0 46.2 %all_gather.7 = bf16[64,1024]{0,1:T(8,128)(2,1)S(1)} all-gather(bf16[64,16]{0,1:T(8,128)(2,1)} %param.14), channel_id=1, replica_groups=mesh['ia'=4,'ja'=8,'ka'=8] {'ja','ka'}, dimensions={1}, use_global_device_ids=true | all-gather | bytes 133120 | tf_op jit(solution)/shard_map/all_gather | solution.py:112
  54.3 1.1 copy.25
  56.3 24.6 %all_gather.6 = bf16[64,512]{0,1:T(8,128)(2,1)S(1)} all-gather(bf16[64,64]{0,1:T(8,128)(2,1)S(1)} %copy.23), channel_id=1, replica_groups=mesh['ia'=4,'ja'=8,'ka'=8] {'ka'}, dimensions={1}, use_global_device_ids=true | all-gather | bytes 73728 | tf_op jit(solution)/shard_map/all_gather | solution.py:113
  81.7 1.6 broadcast_in_dim.7
  83.3 70.1 %while.16 = (s32[]{:T(128)}, f32[64,1024]{1,0:T(8,128)S(1)}, f32[64,512]{1,0:T(8,128)S(1)}, f32[64,1024]{0,1:T(8,128)S(1)}, f32[64,64,64]{2,1,0:T(8,128)}, /*ind...) while((s32[]{:T(128)}, f32[64,1024]{1,0:T(8,128)S(1)}, ...), condition=%wide.region_1.0_spmd, body=%wide.region_0.0_spmd.sunk | while | flops 356534272 | bytes 34849308 | solution.py:101
  88.0 2.1 dynamic-slice_convert_fusion.3
  90.1 2.7 fusion.89
  93.5 0.9 copy-done.1
  95.4 1.0 copy-done.2
  101.9 2.1 dynamic-slice_convert_fusion.3
  104.0 2.7 fusion.89
  107.4 0.9 copy-done.1
  109.3 1.0 copy-done.2
  115.7 2.1 dynamic-slice_convert_fusion.3
  117.9 2.7 fusion.89
  121.3 0.9 copy-done.1
  123.2 1.0 copy-done.2
  129.6 2.1 dynamic-slice_convert_fusion.3
  131.8 2.7 fusion.89
  137.1 1.0 copy-done.2
  143.5 2.1 dynamic-slice_convert_fusion.3
  145.6 2.7 fusion.89
  149.0 0.9 copy-done.1
  150.9 1.0 copy-done.2
  153.4 1.0 copy.28
  155.4 0.9 copy.29
  158.3 179.5 %all-reduce.6.cloned.1.call-done = f32[64,1024]{0,1:T(8,128)} async-done(((f32[64,1024]{0,1:T(8,128)}), f32[64,1024]{0,1:T(8,128)}) %all-reduce.6.cloned.1.call-update) | async-done | bytes 262160
  337.8 1.3 constant_dynamic-slice_fusion.1
  340.0 17.6 %psum.24 = f32[64,64]{1,0:T(8,128)} all-reduce(f32[64,64]{1,0:T(8,128)S(1)} %copy.32), channel_id=1, replica_groups=mesh['ia'=4,'ja'=8,'ka'=8] {'ia'}, use_global_device_ids=true, to_apply=%region_3.0 | all-reduce | flops 4096 | bytes 32768 | tf_op jit(solution)/shard_map/psum | solution.py:129
  357.6 119.0 %psum.25 = f32[64,128]{1,0:T(8,128)} all-reduce(f32[64,128]{1,0:T(8,128)} %reduce-scatter.5.cloned.1.call-done), channel_id=1, replica_groups=mesh['ia'=4,'ja'=8,'ka'=8] {'ia','ja'}, use_global_device_ids=true, to_apply=%region_5.0 | all-reduce | flops 8192 | bytes 65536 | tf_op jit(solution)/shard_map/psum | solution.py:130
  476.6 129.0 %all-reduce.4.cloned.1.call-done = f32[64,64,64]{2,1,0:T(8,128)} async-done(((f32[64,64,64]{2,1,0:T(8,128)}), f32[64,64,64]{2,1,0:T(8,128)}) %all-reduce.4.cloned.1.call-update) | async-done | bytes 1048592 | tf_op jit(solution)/shard_map/psum | solution.py:135
  605.5 3.2 copy.91
  (95 shorter events, 28.5 us)
Async XLA Ops:
  8.0 329.8 %all-reduce.6.cloned.1.call-start = ((), (), s32[]{:S(2)}) async-start(), calls=%async_computation.5 | async-start | bytes 1048576
  54.2 29.1 %copy-start = (bf16[64,64,64]{2,1,0:T(8,128)(2,1)S(1)}, bf16[64,64,64]{2,1,0:T(8,128)(2,1)}, u32[]{:S(2)}) copy-start(bf16[64,64,64]{2,1,0:T(8,128)(2,1)} %param.17) | copy-start | bytes 1572868
  92.8 1.6 copy-start.1
  95.1 1.3 copy-start.2
  106.7 1.6 copy-start.1
  109.0 1.3 copy-start.2
  120.6 1.6 copy-start.1
  122.8 1.3 copy-start.2
  134.4 1.6 copy-start.1
  136.7 1.3 copy-start.2
  148.3 1.6 copy-start.1
  150.6 1.3 copy-start.2
  154.4 2.7 copy-start.3
  154.4 184.7 %reduce-scatter.7.cloned.1.call-start = ((), (), s32[]{:S(2)}) async-start(), calls=%async_computation.4 | async-start | bytes 294912
  155.3 202.3 %reduce-scatter.5.cloned.1.call-start = ((), (), s32[]{:S(2)}) async-start(), calls=%async_computation.3 | async-start | bytes 294912 | tf_op jit(solution)/shard_map/reduce_scatter | solution.py:133
  156.3 449.2 %all-reduce.4.cloned.1.call-start = ((), (), s32[]{:S(2)}) async-start(), calls=%async_computation.2 | async-start | bytes 4194304 | tf_op jit(solution)/shard_map/psum | solution.py:135
Sparse Core Ops, SparseCore 0:
  154.6 183.2 all-reduce.5
  343.8 261.6 all-reduce.3
Sparse Core Ops, SparseCore 1:
  157.4 36.2 reduce-scatter.6
  196.0 35.9 reduce-scatter.4
where the time goes:
time: 617 us; the launch traced here: 616 us
  waiting for transfers between devices  309 us (50%)
  blocking collectives  207 us (34%)
  matrix products  29.4 us (5%)
  local copies, waits for them, and re-layouts  29.1 us (5%)
  between operations  16.2 us (3%)
  loops' own time  14 us (2%)
  other arithmetic  10.7 us (2%)
    unnamed x6, waiting for transfers between devices  180 us
    psum x1, waiting for transfers between devices, on_device(): core_gradient = lax.psum(core_sum, ('ia', 'ja', 'ka'))  129 us
    psum x1, blocking collectives, on_device(): depth_whole = lax.psum(depth_sum, ('ia', 'ja'))  119 us
    all_gather x1, blocking collectives, on_device(): row_table = lax.all_gather(factor_rows, ('ja', 'ka'), axis=1, tiled=True)  46.2 us
    all_gather x1, blocking collectives, on_device(): col_table = lax.all_gather(factor_cols, 'ka', axis=1, tiled=True)  24.6 us
    psum x1, blocking collectives, on_device(): cols_whole = lax.psum(cols_sum, 'ia')  17.6 us
    another operation x1, loops' own time, accumulate_blocks(): return lax.fori_loop(0, live_count, add_slot, start_sums)  14 us
    dot_general x5, matrix products, block_terms(): lax.dot_general(row_factor, second_flat, (((0,), (0,)), ((), ())), prefer...  13.4 us
  transfers between devices with their start and end apart: 4, of which 2 were waited for; matrix products, arithmetic and copies ran while one was open for 1% of the time, Pallas kernels for 0%

commit v1 on v0

--- a/solution.py
+++ b/solution.py
@@ -132,7 +132,7 @@
         lax.psum_scatter(cols_whole, "ka", scatter_dimension=1, tiled=True),
         lax.psum_scatter(depth_whole, "ka", scatter_dimension=1, tiled=True),
     )
-    core_gradient = lax.psum(core_sum, ("ia", "ja", "ka"))
+    core_gradient = lax.psum(lax.psum(core_sum, "ia"), ("ja", "ka"))
     return (rows_gradient, cols_gradient, depth_gradient, core_gradient)
 
 

time: 617 us -> 425 us (0.69)
  waiting for transfers between devices: 309 us -> 120 us
    unnamed x6, waiting for transfers between devices: 180 us -> 59.6 us
    psum x1, waiting for transfers between devices: 129 us -> 59.9 us  [on_device(): core_gradient = lax.psum(lax.psum(core_sum, 'ia'), ('ja', 'ka'))]
where the time goes in v1:
time: 425 us; the launch traced here: 424 us
  blocking collectives  205 us (48%)
  waiting for transfers between devices  120 us (28%)
  matrix products  29.5 us (7%)
  local copies, waits for them, and re-layouts  28.8 us (7%)
  between operations  16.2 us (4%)
  loops' own time  13.6 us (3%)
  other arithmetic  10.7 us (3%)
    psum x1, blocking collectives, on_device(): depth_whole = lax.psum(depth_sum, ('ia', 'ja'))  119 us
    psum x1, waiting for transfers between devices, on_device(): core_gradient = lax.psum(lax.psum(core_sum, 'ia'), ('ja', 'ka'))  59.9 us
    unnamed x6, waiting for transfers between devices  59.6 us
    all_gather x1, blocking collectives, on_device(): row_table = lax.all_gather(factor_rows, ('ja', 'ka'), axis=1, tiled=True)  46.2 us
    all_gather x1, blocking collectives, on_device(): col_table = lax.all_gather(factor_cols, 'ka', axis=1, tiled=True)  24.6 us
    psum x1, blocking collectives, on_device(): cols_whole = lax.psum(cols_sum, 'ia')  15.7 us
    another operation x1, loops' own time, accumulate_blocks(): return lax.fori_loop(0, live_count, add_slot, start_sums)  13.6 us
    dot_general x5, matrix products, block_terms(): lax.dot_general(row_factor, second_flat, (((0,), (0,)), ((), ())), prefer...  13.3 us
  transfers between devices with their start and end apart: 4, of which 2 were waited for; matrix products, arithmetic and copies ran while one was open for 1% of the time, Pallas kernels for 0%

profile of v1, /device:TPU:2, one launch (start us, length us, event | category | flops | bytes accessed | tf_op | source)
XLA Modules:
  0.0 423.7 jit_solution(11345090355918809414)
XLA Ops:
  8.0 46.2 %all_gather.7 = bf16[64,1024]{0,1:T(8,128)(2,1)S(1)} all-gather(bf16[64,16]{0,1:T(8,128)(2,1)} %param.14), channel_id=1, replica_groups=mesh['ia'=4,'ja'=8,'ka'=8] {'ja','ka'}, dimensions={1}, use_global_device_ids=true | all-gather | bytes 133120 | tf_op jit(solution)/shard_map/all_gather | solution.py:112
  54.3 1.1 copy.25
  56.3 24.6 %all_gather.6 = bf16[64,512]{0,1:T(8,128)(2,1)S(1)} all-gather(bf16[64,64]{0,1:T(8,128)(2,1)S(1)} %copy.23), channel_id=1, replica_groups=mesh['ia'=4,'ja'=8,'ka'=8] {'ka'}, dimensions={1}, use_global_device_ids=true | all-gather | bytes 73728 | tf_op jit(solution)/shard_map/all_gather | solution.py:113
  81.7 1.6 broadcast_in_dim.7
  83.3 69.4 %while.16 = (s32[]{:T(128)}, f32[64,1024]{1,0:T(8,128)S(1)}, f32[64,512]{1,0:T(8,128)S(1)}, f32[64,1024]{0,1:T(8,128)S(1)}, f32[64,64,64]{2,1,0:T(8,128)}, /*ind...) while((s32[]{:T(128)}, f32[64,1024]{1,0:T(8,128)S(1)}, ...), condition=%wide.region_1.0_spmd, body=%wide.region_0.0_spmd.sunk | while | flops 356534272 | bytes 34849308 | solution.py:101
  87.9 2.1 dynamic-slice_convert_fusion.3
  90.0 2.7 fusion.89
  93.4 0.9 copy-done.1
  95.3 1.0 copy-done.2
  101.6 2.1 dynamic-slice_convert_fusion.3
  103.8 2.7 fusion.89
  107.1 0.9 copy-done.1
  109.0 1.0 copy-done.2
  115.4 2.1 dynamic-slice_convert_fusion.3
  117.5 2.7 fusion.89
  120.9 0.9 copy-done.1
  122.8 1.0 copy-done.2
  129.1 2.1 dynamic-slice_convert_fusion.3
  131.3 2.7 fusion.89
  134.7 0.9 copy-done.1
  136.6 1.0 copy-done.2
  142.9 2.1 dynamic-slice_convert_fusion.3
  145.0 2.7 fusion.89
  150.3 1.0 copy-done.2
  153.7 0.9 copy.29
  154.7 1.0 copy.28
  155.7 59.9 %all-reduce.5.cloned.1.call-done = f32[64,64,64]{2,1,0:T(8,128)} async-done(((f32[64,64,64]{2,1,0:T(8,128)}), f32[64,64,64]{2,1,0:T(8,128)}) %all-reduce.5.cloned.1.call-update) | async-done | bytes 1048592 | tf_op jit(solution)/shard_map/psum | solution.py:135
  217.8 15.7 %psum.32 = f32[64,64]{1,0:T(8,128)} all-reduce(f32[64,64]{1,0:T(8,128)S(1)} %copy.32), channel_id=1, replica_groups=mesh['ia'=4,'ja'=8,'ka'=8] {'ia'}, use_global_device_ids=true, to_apply=%region_3.0 | all-reduce | flops 4096 | bytes 32768 | tf_op jit(solution)/shard_map/psum | solution.py:129
  233.5 118.7 %psum.33 = f32[64,128]{1,0:T(8,128)} all-reduce(f32[64,128]{1,0:T(8,128)} %reduce-scatter.5.cloned.1.call-done), channel_id=1, replica_groups=mesh['ia'=4,'ja'=8,'ka'=8] {'ia','ja'}, use_global_device_ids=true, to_apply=%region_5.0 | all-reduce | flops 8192 | bytes 65536 | tf_op jit(solution)/shard_map/psum | solution.py:130
  352.3 59.5 %all-reduce.7.cloned.1.call-done = (f32[64,1024]{0,1:T(8,128)}, f32[64,64,64]{2,1,0:T(8,128)}) async-done(((f32[64,1024]{0,1:T(8,128)}, f32[64,64,64]{2,1,0:T(8,128)}), (f32[64,1024]{0,1:T(8,128)}, f32[64,64,64]{2,1,0:T(8,128)})) %all-reduce.7.cloned.1.call-update) | async-done | bytes 1310736
  411.8 1.3 constant_dynamic-slice_fusion.1
  413.1 3.2 copy.92
  (95 shorter events, 27.7 us)
Async XLA Ops:
  8.0 207.7 %all-reduce.5.cloned.1.call-start = ((), (), s32[]{:S(2)}) async-start(), calls=%async_computation.2 | async-start | bytes 4194304 | tf_op jit(solution)/shard_map/psum | solution.py:135
  54.2 29.1 %copy-start = (bf16[64,64,64]{2,1,0:T(8,128)(2,1)S(1)}, bf16[64,64,64]{2,1,0:T(8,128)(2,1)}, u32[]{:S(2)}) copy-start(bf16[64,64,64]{2,1,0:T(8,128)(2,1)} %param.17) | copy-start | bytes 1572868
  92.7 1.6 copy-start.1
  94.9 1.3 copy-start.2
  106.4 1.6 copy-start.1
  108.7 1.3 copy-start.2
  120.2 1.6 copy-start.1
  122.4 1.3 copy-start.2
  133.9 1.6 copy-start.1
  136.2 1.3 copy-start.2
  147.7 1.6 copy-start.1
  150.0 1.3 copy-start.2
  152.8 64.2 %reduce-scatter.7.cloned.1.call-start = ((), (), s32[]{:S(2)}) async-start(), calls=%async_computation.4 | async-start | bytes 294912
  153.7 79.9 %reduce-scatter.5.cloned.1.call-start = ((), (), s32[]{:S(2)}) async-start(), calls=%async_computation.3 | async-start | bytes 294912 | tf_op jit(solution)/shard_map/reduce_scatter | solution.py:133
  153.7 62.0 %copy-start.3 = (u32[256]{0:T(256)S(1)}, u32[256]{0:T(256)}, u32[]{:S(2)}) copy-start(u32[256]{0:T(256)} %constant.44) | copy-start | bytes 3076
  154.7 257.1 %all-reduce.7.cloned.1.call-start = ((), (), s32[]{:S(2)}) async-start(), calls=%async_computation.5 | async-start | bytes 5242880
Sparse Core Ops, SparseCore 0:
  152.9 62.7 all-reduce.4
  219.3 192.4 all-reduce.6
Sparse Core Ops, SparseCore 1:
  155.7 36.1 reduce-scatter.6
  194.2 35.8 reduce-scatter.4
